TPU v7x, 256 devices: a whole 4x4x8 slice. The times are simulated.
256 devices in a mesh: ctx: 32 (over x, y, core), tp: 8 (over z).
Axes of the slice: x: 4, y: 4, z: 8, core: 2. Of those that a mesh axis runs over, the one named last changes fastest.
Arguments:
- queries: bfloat16 [49152, 4096], P('ctx', 'tp'), may hold values from -6 to 6
- keys: bfloat16 [49152, 4096], P('ctx', 'tp'), may hold values from -6 to 6
- values: bfloat16 [49152, 4096], P('ctx', 'tp'), may hold values from -51 to 51, as said below
- out_grad: bfloat16 [49152, 4096], P('ctx', 'tp'), may hold values from -6 to 6
- gain: float32 [4096], P('tp'), may hold values from 0.25 to 1.75
- doc_ids: int32 [192], P('ctx'), may hold values from 0 to 31, never falling along the last dimension, each value on 1 to 96 neighbouring positions
Outputs:
- normed: bfloat16 [49152, 4096], P('ctx', 'tp')
- query_grad: bfloat16 [49152, 4096], P('ctx', 'tp')
- key_grad: bfloat16 [49152, 4096], P('ctx', 'tp')
- value_grad: bfloat16 [49152, 4096], P('ctx', 'tp')
Inputs may be any that keep to these rules, and one draw needn't show every extreme that they name: `doc_ids`: never falls along the sequence; each document covers 1 to max(4, 96) blocks, and one covers exactly that many. `values`: values of order one to ten, with scales that differ from token to token and from feature to feature.
All inputs are finite; a program needn't handle non-finite values.
Results may differ from a plain program's by a relative error of at most 0.0058.
Values sent between devices are 32-bit elements; how exact they have to be, the bound alone decides.
A program may use at most 128 MiB of HBM per device.

v0:
```python
import jax
import jax.numpy as jnp
from jax import lax
from jax.sharding import PartitionSpec as P

HD = 128
C = 256
QW = 4096


epsilon = 1e-06


def carried_in(value, axis, join, neutral, backward):
    count, mine = (lax.axis_size(axis), lax.axis_index(axis))
    pieces = jax.tree.map(lambda part: lax.all_gather(part, axis), value)
    if backward:
        pieces = jax.tree.map(lambda part: part[::-1], pieces)
        mine = count - 1 - mine
    running = jax.tree.map(
        lambda part, zero: jnp.full_like(part, 0) + jnp.asarray(zero, part.dtype), value, neutral
    )

    def lap(position, running):
        longer = join(running, jax.tree.map(lambda part: part[position], pieces))
        return jax.tree.map(lambda new, old: jnp.where(position < mine, new, old), longer, running)

    return lax.fori_loop(0, count - 1, lap, running)


def join_docs(earlier, later):
    early_doc, early_state = earlier
    late_doc, late_state = later
    present = late_doc[0] >= 0.0
    linked = early_doc[0] == late_doc[0]
    joined = jnp.where(present, late_state + jnp.where(linked, early_state, 0.0), early_state)
    return (jnp.where(present, late_doc, early_doc), joined)


def fold_owned(weights, states):
    return jnp.einsum("cj,jhde->chde", weights, states, precision=lax.Precision.HIGHEST)


def local(queries, keys, values, out_grad, gain, doc_ids):
    tok_rows, features = queries.shape
    heads_here = features // HD
    blocks = tok_rows // C
    block_shape = (blocks, C, heads_here, HD)
    query_blk = queries.reshape(block_shape)
    key_blk = keys.reshape(block_shape)
    value_blk = values.reshape(block_shape)
    doc_float = doc_ids.astype(jnp.float32)
    block_pos = jnp.arange(blocks)
    same_doc = doc_float[:, None] == doc_float[None, :]
    causal = jnp.tril(jnp.ones((C, C), dtype=bool))
    nothing_yet = (jnp.full((1,), -1.0, jnp.float32), jnp.zeros((heads_here, HD, HD), jnp.float32))
    block_states = jnp.einsum(
        "nshd,nshe->nhde", key_blk, value_blk, preferred_element_type=jnp.float32
    )
    inside = fold_owned(
        (same_doc & (block_pos[None, :] < block_pos[:, None])).astype(jnp.float32), block_states
    )
    last_doc = doc_float[-1:]
    end_state = fold_owned((doc_float == last_doc)[None, :].astype(jnp.float32), block_states)[0]
    carry_doc, carry_state = carried_in((last_doc, end_state), "ctx", join_docs, nothing_yet, False)
    carry_match = (doc_float == carry_doc).astype(jnp.float32)[:, None, None, None]
    entering = inside + carry_match * carry_state[None]
    state_low = entering.astype(jnp.bfloat16)
    scores = jnp.einsum("nthd,nshd->nhts", query_blk, key_blk, preferred_element_type=jnp.float32)
    scores_low = jnp.where(causal, scores, 0.0).astype(jnp.bfloat16)
    attended = jnp.einsum(
        "nthd,nhde->nthe", query_blk, state_low, preferred_element_type=jnp.float32
    )
    attended = attended + jnp.einsum(
        "nhts,nshe->nthe", scores_low, value_blk, preferred_element_type=jnp.float32
    )
    flat_out = attended.reshape(tok_rows, features)
    weighted = out_grad.astype(jnp.float32) * gain
    total_sq, inner_sum = lax.psum(
        (jnp.sum(flat_out * flat_out, axis=1), jnp.sum(weighted * flat_out, axis=1)), "tp"
    )
    scale_inv = lax.rsqrt(total_sq[:, None] / QW + epsilon)
    normed = (flat_out * scale_inv * gain).astype(jnp.bfloat16)
    mixed_grad = (
        scale_inv * weighted - flat_out * scale_inv**3 * (inner_sum[:, None] / QW)
    ).astype(jnp.bfloat16)
    grad_blk = mixed_grad.reshape(block_shape)
    grad_scores = jnp.einsum(
        "nthe,nshe->nhts", grad_blk, value_blk, preferred_element_type=jnp.float32
    )
    grad_scores = jnp.where(causal, grad_scores, 0.0).astype(jnp.bfloat16)
    query_grad = jnp.einsum(
        "nthe,nhde->nthd", grad_blk, state_low, preferred_element_type=jnp.float32
    )
    query_grad = query_grad + jnp.einsum(
        "nhts,nshd->nthd", grad_scores, key_blk, preferred_element_type=jnp.float32
    )
    grad_states = jnp.einsum(
        "nthd,nthe->nhde", query_blk, grad_blk, preferred_element_type=jnp.float32
    )
    outside = fold_owned(
        (same_doc & (block_pos[None, :] > block_pos[:, None])).astype(jnp.float32), grad_states
    )
    first_doc = doc_float[:1]
    begin_state = fold_owned((doc_float == first_doc)[None, :].astype(jnp.float32), grad_states)[0]
    next_doc, next_state = carried_in((first_doc, begin_state), "ctx", join_docs, nothing_yet, True)
    next_match = (doc_float == next_doc).astype(jnp.float32)[:, None, None, None]
    leaving = outside + next_match * next_state[None]
    leave_low = leaving.astype(jnp.bfloat16)
    key_grad = jnp.einsum(
        "nshe,nhde->nshd", value_blk, leave_low, preferred_element_type=jnp.float32
    )
    key_grad = key_grad + jnp.einsum(
        "nhts,nthd->nshd", grad_scores, query_blk, preferred_element_type=jnp.float32
    )
    value_grad = jnp.einsum(
        "nshd,nhde->nshe", key_blk, leave_low, preferred_element_type=jnp.float32
    )
    value_grad = value_grad + jnp.einsum(
        "nhts,nthe->nshe", scores_low, grad_blk, preferred_element_type=jnp.float32
    )
    return (
        normed,
        query_grad.astype(jnp.bfloat16).reshape(tok_rows, features),
        key_grad.astype(jnp.bfloat16).reshape(tok_rows, features),
        value_grad.astype(jnp.bfloat16).reshape(tok_rows, features),
    )


def solution(mesh):
    return jax.shard_map(
        local,
        mesh=mesh,
        in_specs=(
            P("ctx", "tp"),
            P("ctx", "tp"),
            P("ctx", "tp"),
            P("ctx", "tp"),
            P("tp"),
            P("ctx"),
        ),
        out_specs=(P("ctx", "tp"), P("ctx", "tp"), P("ctx", "tp"), P("ctx", "tp")),
        check_vma=False,
    )
```

profile of v0, /device:TPU:1, one launch (start us, length us, event | category | flops | bytes accessed | tf_op | source)
XLA Modules:
  0.0 479.1 jit_solution(9692971735299035499)
XLA Ops:
  7.2 2.4 reshape.67
  9.6 2.8 reshape.68
  12.5 1.8 fusion.15
  16.2 4.7 fusion.8
  21.0 3.5 reshape.69
  25.2 65.8 %all-reduce.2 = (f32[32]{0:T(128)S(1)}, f32[32]{0:T(128)S(1)}) all-reduce(f32[32]{0:T(128)S(1)} %get-tuple-element.303, f32[32]{0:T(128)S(1)} %slice_dynamic-update-slice_fusion), channel_id=2, replica_groups=mesh['ctx'=32,'tp'=8] {'ctx'}, use_global_device_ids=true, to_apply=%add | all-reduce | flops 64 | bytes 512
  91.0 2.4 select_convert_fusion.1
  95.1 2.9 fusion.26
  98.0 112.8 %while.32 = (s32[]{:T(128)}, f32[1]{0:T(128)}, f32[4,128,128]{2,1,0:T(8,128)S(1)}, s32[]{:T(128)}, f32[32,1]{0,1:T(1,128)S(1)}, /*index=5*/f32[32,4,128,128]{3,2,1,0:T(8,128)}, s32[]{:T(128)}, f32[]{:T(128)}, s32[]{:T(128)}) while((s32[]{:T(128)}, f32[1]{0:T(128)}, f32[4,128,128]{2,1,0:T(8,128)S(1)}, s32[]{:T(128)}, ...), condition=%wide.region_1.2_spmd.clone, body=%wide.region_0.1_spmd.clone.sunk | while | flops 327688 | bytes 786607 | solution.py:28
  210.8 2.1 add_convert_fusion.2
  212.9 4.8 multiply_reduce_fusion
  217.7 3.2 copy.72
  221.0 1.9 fusion.5
  222.9 24.2 %all-reduce.3 = (f32[1536]{0:T(1024)S(1)}, f32[1536]{0:T(1024)S(1)}) all-reduce(f32[1536]{0:T(1024)S(1)} %reduce_sum.21, f32[1536]{0:T(1024)S(1)} %fusion.5), channel_id=1, replica_groups=mesh['ctx'=32,'tp'=8] {'tp'}, use_global_device_ids=true, to_apply=%region_3.4 | all-reduce | flops 3072 | bytes 24576 | tf_op jit(solution)/shard_map/psum | solution.py:79
  247.0 3.6 fusion.4
  250.7 3.5 reshape.71
  254.2 2.7 copy.80
  258.5 2.9 copy.82
  261.4 4.2 fusion.41
  270.9 3.8 copy.79
  274.6 3.0 copy.152
  277.6 2.3 fusion.51
  281.1 2.3 fusion.21
  283.4 45.2 %all-gather.9.cloned.1.call-done = f32[128,128,128]{2,1,0:T(8,128)} async-done(((f32[4,128,128]{2,1,0:T(8,128)}), f32[128,128,128]{2,1,0:T(8,128)}) %all-gather.9.cloned.1.call-update) | async-done | bytes 8388624 | tf_op jit(solution)/shard_map/all_gather | solution.py:16
  328.7 7.7 %rev.7 = f32[32,4,128,128]{3,2,1,0:T(8,128)} reverse(f32[32,4,128,128]{3,2,1,0:T(8,128)} %bitcast.142), dimensions={0} | reverse | bytes 16777216 | tf_op jit(solution)/shard_map/rev | solution.py:18
  336.4 113.0 %while.33 = (s32[]{:T(128)}, f32[1]{0:T(128)}, f32[4,128,128]{2,1,0:T(8,128)S(1)}, s32[]{:T(128)}, f32[32,1]{0,1:T(1,128)S(1)}, /*index=5*/f32[32,4,128,128]{3,2,1,0:T(8,128)}, s32[]{:T(128)}, f32[]{:T(128)}, s32[]{:T(128)}) while((s32[]{:T(128)}, f32[1]{0:T(128)}, f32[4,128,128]{2,1,0:T(8,128)S(1)}, s32[]{:T(128)}, ...), condition=%wide.region_7.8_spmd.clone, body=%wide.region_6.7_spmd.clone.sunk | while | flops 327688 | bytes 786607 | solution.py:28
  449.5 3.8 add_convert_fusion.1
  453.3 2.4 copy.89
  455.7 3.9 fusion.14
  459.6 3.8 copy.92
  463.4 3.0 copy.150
  468.2 2.7 copy.88
  (189 shorter events, 121.2 us)
Async XLA Ops:
  7.2 90.8 %all-gather.7.cloned.1.call-start = ((), (), s32[]{:S(2)}) async-start(), calls=%async_computation | async-start | bytes 8650752 | tf_op jit(solution)/shard_map/all_gather | solution.py:16
  9.6 81.4 %copy-start.2 = (bf16[6,256,4,128]{3,2,1,0:T(4,128)(2,1)}, bf16[6,256,4,128]{3,2,1,0:T(4,128)(2,1)S(1)}, u32[]{:S(2)}) copy-start(bf16[6,256,4,128]{3,2,1,0:T(4,128)(2,1)S(1)} %reshape.67) | copy-start | bytes 4718596
  9.6 2.8 copy-start.18
  12.4 81.0 %copy-start = (bf16[6,256,4,128]{3,2,1,0:T(4,128)(2,1)}, bf16[6,256,4,128]{3,2,1,0:T(4,128)(2,1)S(1)}, u32[]{:S(2)}) copy-start(bf16[6,256,4,128]{3,2,1,0:T(4,128)(2,1)S(1)} %reshape.68) | copy-start | bytes 4718596
  12.5 1.9 copy-start.19
  20.9 307.8 %all-gather.9.cloned.1.call-start = ((), (), s32[]{:S(2)}) async-start(), calls=%async_computation.1 | async-start | bytes 8650752 | tf_op jit(solution)/shard_map/all_gather | solution.py:16
  93.4 1.6 copy-start.8
  95.1 115.7 %copy-start.10 = (f32[6,4,128,128]{3,2,1,0:T(8,128)S(1)}, f32[6,4,128,128]{3,2,1,0:T(8,128)}, u32[]{:S(2)}) copy-start(f32[6,4,128,128]{3,2,1,0:T(8,128)} %fusion.15) | copy-start | bytes 4718596
  210.8 2.1 copy-start.5
  212.9 4.8 copy-start.15
  217.7 3.3 copy-start.17
  254.1 2.7 copy-start.6
  261.4 4.3 copy-start.1
  265.7 1.4 copy-start.3
  267.1 1.6 copy-start.12
  267.1 2.0 copy-start.16
  274.6 3.0 copy-start.9
  277.6 2.3 copy-start.7
  277.6 3.5 copy-start.13
  453.3 2.4 copy-start.4
  459.6 6.8 %copy-start.14 = (bf16[6,4,128,128]{2,3,1,0:T(8,128)(2,1)S(1)}, bf16[6,4,128,128]{2,3,1,0:T(8,128)(2,1)}, u32[]{:S(2)}) copy-start(bf16[6,4,128,128]{2,3,1,0:T(8,128)(2,1)} %copy.89) | copy-start | bytes 2359300
  463.4 3.0 copy-start.11
Sparse Core Ops, SparseCore 0:
  21.0 62.2 all-gather.6
  265.7 62.9 all-gather.8
where the time goes:
time: 484 us; the launch traced here: 479 us
  loops' own time  121 us (25%)
  local copies, waits for them, and re-layouts  93.7 us (19%)
  blocking collectives  89.9 us (19%)
  other arithmetic  72.7 us (15%)
  waiting for transfers between devices  45.3 us (9%)
  matrix products  42.6 us (9%)
  between operations  14.3 us (3%)
    another operation x2, loops' own time, carried_in(): return lax.fori_loop(0, count - 1, lap, running)  121 us
    select_n x62, other arithmetic, lap(): jnp.where(position < mine, new, old)  67.1 us
    unnamed x1, blocking collectives  65.8 us
    all_gather x2, waiting for transfers between devices, carried_in(): pieces = jax.tree.map(lambda part: lax.all_gather(part, axis), value)  45.2 us
    dynamic_slice x62, local copies, waits for them, and re-layouts, lap(): longer = join(running, jax.tree.map(lambda part: part[position], pieces))  38.2 us
    psum x1, blocking collectives, local(): lax.psum((jnp.sum(flat_out * flat_out, axis=1), jnp.sum(weighted * flat_o...  24.2 us
    dot_general x4, matrix products, fold_owned(): jnp.einsum('cj,jhde->chde', weights, states, precision=lax.Precision.HIGH...  14.7 us
    unnamed x48, local copies, waits for them, and re-layouts  12.9 us
  transfers between devices with their start and end apart: 2, of which 1 were waited for; matrix products, arithmetic and copies ran while one was open for 5% of the time, Pallas kernels for 0%

commit v1 on v0

v1 whole, which is shorter than its diff:
```python
import functools

import jax
import jax.numpy as jnp
from jax import lax
from jax.experimental import pallas as pl
from jax.experimental.pallas import tpu as pltpu
from jax.sharding import PartitionSpec as P

HD = 128
C = 256
epsilon = 1e-06

MESH = pl.DeviceIdType.MESH
F32 = jnp.float32
BF16 = jnp.bfloat16


def mm(a, b, dims):
    return lax.dot_general(a, b, (dims, ((), ())), preferred_element_type=F32)


NN = ((1,), (0,))
NT = ((1,), (1,))
TN = ((0,), (0,))


def kernel(
    NC, NT_, NB, NH, QW,
    doc_ref, q_hbm, k_hbm, v_hbm, g_hbm, gain_ref,
    normed_hbm, qg_hbm, kg_hbm, vg_hbm,
    q_ref, k_ref, v_ref, g_ref,
    sc_ref, att_ref, d_ref, state_ref, enter_ref, leave_ref, kp_ref, vp_ref,
    o_norm, o_qg, o_kg, o_vg,
    docrow, docs,
    f_end, f_in, f_out, f_carry,
    b_end, b_in, b_out, b_carry,
    stat_send, stat_in,
    load_sem, store_sem, send_sem, doc_sem, f1_sem, f2_sem, b1_sem, b2_sem,
    tsend_sem, trecv_sem,
):
    PR = NH * HD // NC
    HP = HD // PR
    W = NH * HD
    me = lax.axis_index("ctx")
    mt = lax.axis_index("tp")

    def rows(n):
        return pl.ds(pl.multiple_of(n * C, C), C)

    def cols(h):
        return slice(h * HD, (h + 1) * HD)

    def load(i, hbm, ref, n):
        return pltpu.make_async_copy(hbm.at[rows(n)], ref.at[rows(n)], load_sem.at[i, n])

    loads = ((k_hbm, k_ref), (v_hbm, v_ref), (q_hbm, q_ref), (g_hbm, g_ref))

    barrier = pltpu.get_barrier_semaphore()

    @pl.loop(1, NC)
    def _(i):
        pl.semaphore_signal(
            barrier, inc=1, device_id={"ctx": lax.rem(me + i, NC)}, device_id_type=MESH
        )

    @pl.loop(1, NT_)
    def _(i):
        pl.semaphore_signal(
            barrier, inc=1, device_id={"tp": lax.rem(mt + i, NT_)}, device_id_type=MESH
        )

    @pl.loop(0, NB)
    def _(n):
        load(0, k_hbm, k_ref, n).start()
        load(1, v_hbm, v_ref, n).start()

    @pl.loop(0, NB)
    def _(n):
        load(2, q_hbm, q_ref, n).start()

    @pl.loop(0, NB)
    def _(n):
        load(3, g_hbm, g_ref, n).start()

    half = lax.broadcasted_iota(jnp.int32, (2, 128), 0)
    my_docs = jnp.where(half == 0, doc_ref[0], doc_ref[NB - 1]).astype(F32)
    docrow[...] = my_docs
    docs[me] = my_docs

    pl.semaphore_wait(barrier, NC - 1 + NT_ - 1)

    def exchange(i, src, dst, recv):
        return pltpu.make_async_remote_copy(
            src_ref=src,
            dst_ref=dst,
            send_sem=send_sem.at[i],
            recv_sem=recv.at[i],
            device_id={"ctx": lax.rem(me + i, NC)},
            device_id_type=MESH,
        )

    def doc_copy(i):
        return exchange(i, docrow, docs.at[me], doc_sem)

    @pl.loop(1, NC)
    def _(i):
        doc_copy(i).start()

    def f1_copy(i):
        return exchange(i, f_end.at[lax.rem(me + i, NC)], f_in.at[me], f1_sem)

    def f2_copy(i):
        return exchange(i, f_out.at[lax.rem(me + i, NC)], f_carry.at[me], f2_sem)

    def b1_copy(i):
        return exchange(i, b_end.at[lax.rem(me + i, NC)], b_in.at[me], b1_sem)

    def b2_copy(i):
        return exchange(i, b_out.at[lax.rem(me + i, NC)], b_carry.at[me], b2_sem)

    def start_all(copy):
        @pl.loop(1, NC)
        def _(i):
            copy(i).start()

    def wait_send(copy):
        @pl.loop(1, NC)
        def _(i):
            copy(i).wait_send()

    def wait_recv(copy):
        @pl.loop(1, NC)
        def _(i):
            copy(i).wait_recv()

    def same(a, b):
        return jnp.where(doc_ref[a] == doc_ref[b], 1.0, 0.0).astype(F32)

    def piece(h):
        return pl.ds(h * HP, HP)

    @pl.loop(0, NB)
    def _(n):
        load(0, k_hbm, k_ref, n).wait()
        load(1, v_hbm, v_ref, n).wait()
        prev = jnp.maximum(n - 1, 0)
        link = jnp.where(n > 0, same(prev, n), 0.0)
        for h in range(NH):
            kv = mm(k_ref[rows(n), cols(h)], v_ref[rows(n), cols(h)], TN).reshape(HP, PR, HD)
            run = jnp.where(link > 0.0, f_end[piece(h)], 0.0)
            state_ref[n, piece(h)] = run
            f_end[piece(h)] = run + kv

    wait_send(doc_copy)
    start_all(f1_copy)
    f_in[me] = f_end[me]

    causal = lax.broadcasted_iota(jnp.int32, (C, C), 0) >= lax.broadcasted_iota(
        jnp.int32, (C, C), 1
    )

    def inner(n):
        load(2, q_hbm, q_ref, n).wait()
        for h in range(NH):
            q = q_ref[rows(n), cols(h)]
            s = mm(q, k_ref[rows(n), cols(h)], NT)
            s = jnp.where(causal, s, 0.0).astype(BF16)
            sc_ref[n * NH + h] = s
            att_ref[rows(n), cols(h)] = mm(s, v_ref[rows(n), cols(h)], NN)

    @pl.loop(0, NB // 2)
    def _(n):
        inner(n)

    wait_recv(doc_copy)
    wait_recv(f1_copy)

    def fwd_step(j, run):
        before = jnp.maximum(j - 2, 0)
        last = docs[j - 1, 1:2, :]
        run = f_in[j - 1] + jnp.where((docs[before, 1:2, :] == last) & (j >= 2), run, 0.0)
        f_out[j] = jnp.where(last == docs[j, 0:1, :], run, 0.0)
        return run

    f_out[0] = jnp.zeros((PR, HD), F32)
    lax.fori_loop(1, NC, fwd_step, jnp.zeros((PR, HD), F32))
    wait_send(f1_copy)
    start_all(f2_copy)
    f_carry[me] = f_out[me]

    @pl.loop(NB // 2, NB)
    def _(n):
        inner(n)

    @pl.loop(0, NB)
    def _(n):
        load(3, g_hbm, g_ref, n).wait()

    wait_recv(f2_copy)

    gain = gain_ref[...]
    lane = lax.broadcasted_iota(jnp.int32, (C, 128), 1)
    stat = jnp.zeros((C, 128), F32)
    for n in range(NB):
        match = jnp.where(doc_ref[n] == doc_ref[0], 1.0, 0.0).astype(F32)
        sq = jnp.zeros((C, HD), F32)
        inn = jnp.zeros((C, HD), F32)
        for h in range(NH):
            enter = state_ref[n, piece(h)] + match * f_carry[piece(h)]
            enter = enter.reshape(HD, HD).astype(BF16)
            enter_ref[n, h] = enter
            att = att_ref[rows(n), cols(h)] + mm(q_ref[rows(n), cols(h)], enter, NN)
            att_ref[rows(n), cols(h)] = att
            sq = sq + att * att
            inn = inn + (g_ref[rows(n), cols(h)].astype(F32) * gain[:, cols(h)]) * att
        stat = jnp.where(lane == n, jnp.sum(sq, axis=1, keepdims=True), stat)
        stat = jnp.where(lane == 8 + n, jnp.sum(inn, axis=1, keepdims=True), stat)
    stat_t = jnp.transpose(stat)[0:16]
    stat_send[...] = stat_t
    stat_in[mt] = stat_t

    def t_copy(i):
        return pltpu.make_async_remote_copy(
            src_ref=stat_send,
            dst_ref=stat_in.at[mt],
            send_sem=tsend_sem.at[i],
            recv_sem=trecv_sem.at[i],
            device_id={"tp": lax.rem(mt + i, NT_)},
            device_id_type=MESH,
        )

    @pl.loop(1, NT_)
    def _(i):
        t_copy(i).start()

    wait_send(f2_copy)

    @pl.loop(1, NT_)
    def _(i):
        t_copy(i).wait()

    total = stat_in[0]
    for i in range(1, NT_):
        total = total + stat_in[i]
    r = lax.rsqrt(total[0:8] / QW + epsilon)
    coef = r * r * r * (total[8:16] / QW)
    packed = jnp.concatenate([r, coef, jnp.zeros((112, C), F32)], axis=0)
    columns = jnp.transpose(packed)

    for n in reversed(range(NB)):
        rc = columns[:, n : n + 1]
        cc = columns[:, 8 + n : 9 + n]
        for h in range(NH):
            att = att_ref[rows(n), cols(h)]
            w = g_ref[rows(n), cols(h)].astype(F32) * gain[:, cols(h)]
            d = (rc * w - att * cc).astype(BF16)
            d_ref[rows(n), cols(h)] = d
            o_norm[rows(n), cols(h)] = (att * rc * gain[:, cols(h)]).astype(BF16)
            qd = mm(q_ref[rows(n), cols(h)], d, TN).reshape(HP, PR, HD)
            if n == NB - 1:
                run = jnp.zeros((HP, PR, HD), F32)
            else:
                run = jnp.where(same(n, n + 1) > 0.0, b_end[piece(h)], 0.0)
            leave_ref[n, piece(h)] = run
            b_end[piece(h)] = run + qd

    start_all(b1_copy)
    b_in[me] = b_end[me]

    def store(i, ref, hbm, n):
        return pltpu.make_async_copy(ref.at[rows(n)], hbm.at[rows(n)], store_sem.at[i, n])

    def outer(n):
        store(0, o_norm, normed_hbm, n).start()
        for h in range(NH):
            q = q_ref[rows(n), cols(h)]
            d = d_ref[rows(n), cols(h)]
            gs = mm(d, v_ref[rows(n), cols(h)], NT)
            gs = jnp.where(causal, gs, 0.0).astype(BF16)
            qg = mm(d, enter_ref[n, h], NT) + mm(gs, k_ref[rows(n), cols(h)], NN)
            o_qg[rows(n), cols(h)] = qg.astype(BF16)
            kp_ref[rows(n), cols(h)] = mm(gs, q, TN)
            vp_ref[rows(n), cols(h)] = mm(sc_ref[n * NH + h], d, TN)
        store(1, o_qg, qg_hbm, n).start()

    @pl.loop(0, NB // 2)
    def _(n):
        outer(n)

    wait_recv(b1_copy)

    def bwd_step(t, run):
        j = NC - 1 - t
        after = jnp.minimum(j + 2, NC - 1)
        first = docs[j + 1, 0:1, :]
        run = b_in[j + 1] + jnp.where((docs[after, 0:1, :] == first) & (t >= 2), run, 0.0)
        b_out[j] = jnp.where(first == docs[j, 1:2, :], run, 0.0)
        return run

    b_out[NC - 1] = jnp.zeros((PR, HD), F32)
    lax.fori_loop(1, NC, bwd_step, jnp.zeros((PR, HD), F32))
    wait_send(b1_copy)
    start_all(b2_copy)
    b_carry[me] = b_out[me]

    @pl.loop(NB // 2, NB)
    def _(n):
        outer(n)

    wait_recv(b2_copy)

    @pl.loop(0, NB)
    def _(n):
        match = same(n, NB - 1)
        for h in range(NH):
            leave = leave_ref[n, piece(h)] + match * b_carry[piece(h)]
            leave = leave.reshape(HD, HD).astype(BF16)
            kg = kp_ref[rows(n), cols(h)] + mm(v_ref[rows(n), cols(h)], leave, NT)
            o_kg[rows(n), cols(h)] = kg.astype(BF16)
            vg = vp_ref[rows(n), cols(h)] + mm(k_ref[rows(n), cols(h)], leave, NN)
            o_vg[rows(n), cols(h)] = vg.astype(BF16)
        store(2, o_kg, kg_hbm, n).start()
        store(3, o_vg, vg_hbm, n).start()

    wait_send(b2_copy)

    @pl.loop(0, NB)
    def _(n):
        store(0, o_norm, normed_hbm, n).wait()
        store(1, o_qg, qg_hbm, n).wait()
        store(2, o_kg, kg_hbm, n).wait()
        store(3, o_vg, vg_hbm, n).wait()


def local(NC, NT_, queries, keys, values, out_grad, gain, doc_ids):
    tok, W = queries.shape
    NB, NH = tok // C, W // HD
    PR = NH * HD // NC
    QW = W * NT_
    any_spec = pl.BlockSpec(memory_space=pl.ANY)
    out = jax.ShapeDtypeStruct((tok, W), BF16)
    dma = pltpu.SemaphoreType.DMA
    ring = [pltpu.VMEM((NC, PR, HD), F32)] * 4
    return pl.pallas_call(
        functools.partial(kernel, NC, NT_, NB, NH, QW),
        out_shape=(out,) * 4,
        in_specs=[pl.BlockSpec(memory_space=pltpu.SMEM)]
        + [any_spec] * 4
        + [pl.BlockSpec(memory_space=pltpu.VMEM)],
        out_specs=(any_spec,) * 4,
        scratch_shapes=[pltpu.VMEM((tok, W), BF16)] * 4
        + [
            pltpu.VMEM((NB * NH, C, C), BF16),
            pltpu.VMEM((tok, W), F32),
            pltpu.VMEM((tok, W), BF16),
            pltpu.VMEM((NB, NC, PR, HD), F32),
            pltpu.VMEM((NB, NH, HD, HD), BF16),
            pltpu.VMEM((NB, NC, PR, HD), F32),
            pltpu.VMEM((tok, W), F32),
            pltpu.VMEM((tok, W), F32),
        ]
        + [pltpu.VMEM((tok, W), BF16)] * 4
        + [pltpu.VMEM((2, 128), F32), pltpu.VMEM((NC, 2, 128), F32)]
        + ring
        + ring
        + [
            pltpu.VMEM((16, C), F32),
            pltpu.VMEM((NT_, 16, C), F32),
            dma((4, NB)),
            dma((4, NB)),
            dma((NC,)),
            dma((NC,)),
            dma((NC,)),
            dma((NC,)),
            dma((NC,)),
            dma((NC,)),
            dma((NT_,)),
            dma((NT_,)),
        ],
        compiler_params=pltpu.CompilerParams(
            collective_id=0, has_side_effects=True, vmem_limit_bytes=60 * 2**20
        ),
        name="packed_linear_attention",
    )(doc_ids, queries, keys, values, out_grad, gain.reshape(1, W))


def solution(mesh):
    ctx, tp = mesh.shape["ctx"], mesh.shape["tp"]
    return jax.shard_map(
        functools.partial(local, ctx, tp),
        mesh=mesh,
        in_specs=(
            P("ctx", "tp"),
            P("ctx", "tp"),
            P("ctx", "tp"),
            P("ctx", "tp"),
            P("tp"),
            P("ctx"),
        ),
        out_specs=(P("ctx", "tp"), P("ctx", "tp"), P("ctx", "tp"), P("ctx", "tp")),
        check_vma=False,
    )
```

time: 484 us -> 63.9 us (0.13)
  loops' own time: 121 us -> 0 us
  blocking collectives: 89.9 us -> 0 us
  local copies, waits for them, and re-layouts: 93.7 us -> 7.87 us
  other arithmetic: 72.7 us -> 0 us
  Pallas kernels: 0 us -> 55.2 us
  waiting for transfers between devices: 45.3 us -> 0 us
  matrix products: 42.6 us -> 0 us
  between operations: 14.3 us -> 0.65 us
    another operation x2 -> x0, loops' own time: 121 us -> none  [carried_in(): return lax.fori_loop(0, count - 1, lap, running)]
    select_n x62 -> x0, other arithmetic: 67.1 us -> none  [lap(): jnp.where(position < mine, new, old)]
    unnamed x1 -> x0, blocking collectives: 65.8 us -> none
    pallas_call x0 -> x1, Pallas kernels: none -> 55.2 us  [local(): pl.pallas_call(functools.partial(kernel, NC, NT_, NB, NH, QW), out_shape=...]
    all_gather x2 -> x0, waiting for transfers between devices: 45.2 us -> none  [carried_in(): pieces = jax.tree.map(lambda part: lax.all_gather(part, axis), value)]
    dot_general x16 -> x0, matrix products: 42.6 us -> none  [the longest x4 14.7 us: fold_owned(): jnp.einsum('cj,jhde->chde', weights, states, precision=lax.Precision.HIGH...]
    dynamic_slice x62 -> x0, local copies, waits for them, and re-layouts: 38.2 us -> none  [lap(): longer = join(running, jax.tree.map(lambda part: part[position], pieces))]
    psum x1 -> x0, blocking collectives: 24.2 us -> none  [local(): lax.psum((jnp.sum(flat_out * flat_out, axis=1), jnp.sum(weighted * flat_o...]
  transfers between devices with their start and end apart: 2 -> 0, of which waited for: 1 -> 0; matrix products, arithmetic and copies ran while one was open for 5% -> 0% of each run, Pallas kernels for 0% -> 0%
where the time goes in v1:
time: 63.9 us; the launch traced here: 63.7 us
  Pallas kernels  55.2 us (86%)
  local copies, waits for them, and re-layouts  7.87 us (12%)
  between operations  0.65 us (1%)
    pallas_call x1, Pallas kernels, local(): pl.pallas_call(functools.partial(kernel, NC, NT_, NB, NH, QW), out_shape=...  55.2 us
    unnamed x10, local copies, waits for them, and re-layouts  7.87 us

profile of v1, /device:TPU:1, one launch (start us, length us, event | category | flops | bytes accessed | tf_op | source)
XLA Modules:
  0.0 63.7 jit_solution(12607495148557818475)
XLA Ops:
  0.6 55.2 %packed_linear_attention.1 = (bf16[1536,512]{1,0:T(8,128)(2,1)}, bf16[1536,512]{1,0:T(8,128)(2,1)}, bf16[1536,512]{1,0:T(8,128)(2,1)}, bf16[1536,512]{1,0:T(8,128)(2,1)}) custom-call(s32[6]{0:T(128)} %doc_ref.1, bf16[1536,512]{1,0:T(8,128)(2,1)} %q_hbm.1, bf16[1536,512]{1,0:T(8,128)(2,1)} %k_hbm.1, bf16[1536,512]{1,0:T(8,128)(2,1)} %v_hbm.1, ...), custom_call_target="tpu_custom_call" | custom-call | tf_op jit(solution)/shard_map/packed_linear_attention/pallas_call | solution.py:345
  55.8 0.0 copy-start.2
  55.9 2.8 %copy.14 = bf16[1536,512]{1,0:T(8,128)(2,1)} copy(bf16[1536,512]{1,0:T(8,128)(2,1)} %get-tuple-element.8) | data formatting | bytes 3145728
  58.6 0.0 copy-done.2
  58.6 0.0 copy-start.1
  58.6 1.1 %copy.15 = bf16[1536,512]{1,0:T(8,128)(2,1)} copy(bf16[1536,512]{1,0:T(8,128)(2,1)S(1)} %copy-done.2) | data formatting | bytes 3145728
  59.8 0.8 %copy-done.1 = bf16[1536,512]{1,0:T(8,128)(2,1)S(1)} copy-done((bf16[1536,512]{1,0:T(8,128)(2,1)S(1)}, bf16[1536,512]{1,0:T(8,128)(2,1)}, u32[]{:S(2)}) %copy-start.1) | copy-done | bytes 1572888
  60.6 0.0 copy-start
  60.6 1.1 %copy.16 = bf16[1536,512]{1,0:T(8,128)(2,1)} copy(bf16[1536,512]{1,0:T(8,128)(2,1)S(1)} %copy-done.1) | data formatting | bytes 3145728
  61.8 0.8 %copy-done = bf16[1536,512]{1,0:T(8,128)(2,1)S(1)} copy-done((bf16[1536,512]{1,0:T(8,128)(2,1)S(1)}, bf16[1536,512]{1,0:T(8,128)(2,1)}, u32[]{:S(2)}) %copy-start) | copy-done | bytes 1572888
  62.6 1.1 %copy.17 = bf16[1536,512]{1,0:T(8,128)(2,1)} copy(bf16[1536,512]{1,0:T(8,128)(2,1)S(1)} %copy-done) | data formatting | bytes 3145728
Async XLA Ops:
  55.8 2.8 %copy-start.2 = (bf16[1536,512]{1,0:T(8,128)(2,1)S(1)}, bf16[1536,512]{1,0:T(8,128)(2,1)}, u32[]{:S(2)}) copy-start(bf16[1536,512]{1,0:T(8,128)(2,1)} %get-tuple-element.9) | copy-start | bytes 4718596
  58.6 2.0 %copy-start.1 = (bf16[1536,512]{1,0:T(8,128)(2,1)S(1)}, bf16[1536,512]{1,0:T(8,128)(2,1)}, u32[]{:S(2)}) copy-start(bf16[1536,512]{1,0:T(8,128)(2,1)} %get-tuple-element.10) | copy-start | bytes 4718596
  60.6 2.0 %copy-start = (bf16[1536,512]{1,0:T(8,128)(2,1)S(1)}, bf16[1536,512]{1,0:T(8,128)(2,1)}, u32[]{:S(2)}) copy-start(bf16[1536,512]{1,0:T(8,128)(2,1)} %get-tuple-element.11) | copy-start | bytes 4718596

commit v2 on v1

v2 whole, which is shorter than its diff:
```python
import functools

import jax
import jax.numpy as jnp
from jax import lax
from jax.experimental import pallas as pl
from jax.experimental.pallas import tpu as pltpu
from jax.sharding import PartitionSpec as P

HD = 128
C = 256
epsilon = 1e-06

MESH = pl.DeviceIdType.MESH
F32 = jnp.float32
BF16 = jnp.bfloat16


def mm(a, b, dims):
    return lax.dot_general(a, b, (dims, ((), ())), preferred_element_type=F32)


NN = ((1,), (0,))
NT = ((1,), (1,))
TN = ((0,), (0,))


def kernel(
    NC, NT_, NB, NH, QW,
    doc_ref, q_hbm, k_hbm, v_hbm, g_hbm, gain_ref,
    o_norm, o_qg, kp_ref, vp_ref, low_ref, k_ref, v_ref,
    q_ref, g_ref,
    sc_ref, att_ref, d_ref, state_ref, enter_ref, leave_ref,
    docrow, docs,
    f_end, f_in, f_out, f_carry, f_swap, f_chip, f_give,
    b_end, b_in, b_out, b_carry, b_swap, b_chip, b_give,
    stat_send, stat_in,
    load_sem, send_sem, doc_sem, f1_sem, f2_sem, b1_sem, b2_sem,
    swap_send, swap_recv,
    tsend_sem, trecv_sem,
):
    PR = NH * HD // NC
    HP = HD // PR
    W = NH * HD
    NP = NC // 2
    HH = NH // 2
    me = lax.axis_index("ctx")
    mt = lax.axis_index("tp")
    core = lax.rem(me, 2)
    chip = me // 2
    other = 1 - core

    def rows(n):
        return pl.ds(pl.multiple_of(n * C, C), C)

    def cols(h):
        if isinstance(h, int):
            return slice(h * HD, (h + 1) * HD)
        return pl.ds(pl.multiple_of(h * HD, HD), HD)

    def load(i, hbm, ref, n):
        return pltpu.make_async_copy(hbm.at[rows(n)], ref.at[rows(n)], load_sem.at[i, n])

    loads = ((k_hbm, k_ref), (v_hbm, v_ref), (q_hbm, q_ref), (g_hbm, g_ref))

    barrier = pltpu.get_barrier_semaphore()

    @pl.loop(1, NC)
    def _(i):
        pl.semaphore_signal(
            barrier, inc=1, device_id={"ctx": lax.rem(me + i, NC)}, device_id_type=MESH
        )

    @pl.loop(1, NT_)
    def _(i):
        pl.semaphore_signal(
            barrier, inc=1, device_id={"tp": lax.rem(mt + i, NT_)}, device_id_type=MESH
        )

    @pl.loop(0, NB)
    def _(n):
        load(0, k_hbm, k_ref, n).start()
        load(1, v_hbm, v_ref, n).start()

    @pl.loop(0, NB)
    def _(n):
        load(2, q_hbm, q_ref, n).start()

    @pl.loop(0, NB)
    def _(n):
        load(3, g_hbm, g_ref, n).start()

    half = lax.broadcasted_iota(jnp.int32, (2, 128), 0)
    my_docs = jnp.where(half == 0, doc_ref[0], doc_ref[NB - 1]).astype(F32)
    docrow[...] = my_docs
    docs[me] = my_docs

    pl.semaphore_wait(barrier, NC - 1 + NT_ - 1)

    def exchange(i, src, dst, recv):
        return pltpu.make_async_remote_copy(
            src_ref=src,
            dst_ref=dst,
            send_sem=send_sem.at[i],
            recv_sem=recv.at[i],
            device_id={"ctx": lax.rem(me + i, NC)},
            device_id_type=MESH,
        )

    def doc_copy(i):
        return exchange(i, docrow, docs.at[me], doc_sem)

    @pl.loop(1, NC)
    def _(i):
        doc_copy(i).start()

    def chips(i, src, dst, recv):
        return pltpu.make_async_remote_copy(
            src_ref=src,
            dst_ref=dst,
            send_sem=send_sem.at[i],
            recv_sem=recv.at[i],
            device_id={"ctx": lax.rem(chip + i, NP) * 2 + core},
            device_id_type=MESH,
        )

    def f1_copy(i):
        return chips(i, f_chip.at[lax.rem(chip + i, NP)], f_in.at[chip], f1_sem)

    def f2_copy(i):
        return chips(i, f_out.at[lax.rem(chip + i, NP)], f_carry.at[core * NP + chip], f2_sem)

    def b1_copy(i):
        return chips(i, b_chip.at[lax.rem(chip + i, NP)], b_in.at[chip], b1_sem)

    def b2_copy(i):
        return chips(i, b_out.at[lax.rem(chip + i, NP)], b_carry.at[core * NP + chip], b2_sem)

    def swap(i, src, dst):
        return pltpu.make_async_remote_copy(
            src_ref=src,
            dst_ref=dst,
            send_sem=swap_send.at[i],
            recv_sem=swap_recv.at[i],
            device_id={"ctx": chip * 2 + other},
            device_id_type=MESH,
        )

    mine = pl.ds(core * NP, NP)
    theirs = pl.ds(other * NP, NP)
    f_swap_in = swap(0, f_end.at[theirs], f_swap)
    f_swap_out = swap(1, f_give, f_carry.at[mine])
    b_swap_in = swap(2, b_end.at[theirs], b_swap)
    b_swap_out = swap(3, b_give, b_carry.at[mine])

    def start_all(copy, count):
        @pl.loop(1, count)
        def _(i):
            copy(i).start()

    def wait_send(copy, count):
        @pl.loop(1, count)
        def _(i):
            copy(i).wait_send()

    def wait_recv(copy, count):
        @pl.loop(1, count)
        def _(i):
            copy(i).wait_recv()

    def same(a, b):
        return jnp.where(doc_ref[a] == doc_ref[b], 1.0, 0.0).astype(F32)

    def piece(h):
        return pl.ds(h * HP, HP)

    def states(n, first):
        prev = jnp.maximum(n - 1, 0)
        link = jnp.where(n > 0, same(prev, n), 0.0)
        for i in range(HH):
            h = first + i
            kv = mm(k_ref[rows(n), cols(h)], v_ref[rows(n), cols(h)], TN).reshape(HP, PR, HD)
            run = jnp.where(link > 0.0, f_end[piece(h)], 0.0)
            state_ref[n, piece(h)] = run
            f_end[piece(h)] = run + kv

    @pl.loop(0, NB)
    def _(n):
        load(0, k_hbm, k_ref, n).wait()
        load(1, v_hbm, v_ref, n).wait()
        states(n, other * HH)

    f_swap_in.start()

    @pl.loop(0, NB)
    def _(n):
        states(n, core * HH)

    wait_send(doc_copy, NC)
    wait_recv(doc_copy, NC)
    first0, last0 = docs[chip * 2, 0:1, :], docs[chip * 2, 1:2, :]
    first1, last1 = docs[chip * 2 + 1, 0:1, :], docs[chip * 2 + 1, 1:2, :]
    is0 = core == 0

    def choose(cond, x):
        return jnp.where(cond, x, 0.0)

    f_swap_in.wait_recv()

    @pl.loop(0, NP)
    def _(i):
        own, got = f_end[core * NP + i], f_swap[i]
        e0, e1 = jnp.where(is0, own, got), jnp.where(is0, got, own)
        f_chip[i] = e1 + choose(last0 == last1, e0)

    start_all(f1_copy, NP)
    f_in[chip] = f_chip[chip]

    causal = lax.broadcasted_iota(jnp.int32, (C, C), 0) >= lax.broadcasted_iota(
        jnp.int32, (C, C), 1
    )

    def inner(n):
        load(2, q_hbm, q_ref, n).wait()
        for h in range(NH):
            q = q_ref[rows(n), cols(h)]
            s = mm(q, k_ref[rows(n), cols(h)], NT)
            s = jnp.where(causal, s, 0.0).astype(BF16)
            sc_ref[n * NH + h] = s
            att_ref[rows(n), cols(h)] = mm(s, v_ref[rows(n), cols(h)], NN)

    @pl.loop(0, NB // 2)
    def _(n):
        inner(n)

    wait_recv(f1_copy, NP)

    def fwd_step(j, run):
        before = jnp.maximum(j - 2, 0)
        last = docs[2 * j - 1, 1:2, :]
        run = f_in[j - 1] + choose((docs[2 * before + 1, 1:2, :] == last) & (j >= 2), run)
        f_out[j] = choose(last == docs[2 * j, 0:1, :], run)
        return run

    f_out[0] = jnp.zeros((PR, HD), F32)
    lax.fori_loop(1, NP, fwd_step, jnp.zeros((PR, HD), F32))
    wait_send(f1_copy, NP)
    start_all(f2_copy, NP)
    f_carry[core * NP + chip] = f_out[chip]

    @pl.loop(NB // 2, NB)
    def _(n):
        inner(n)

    @pl.loop(0, NB)
    def _(n):
        load(3, g_hbm, g_ref, n).wait()

    wait_recv(f2_copy, NP)

    @pl.loop(0, NP)
    def _(i):
        x = f_carry[core * NP + i]
        e0 = jnp.where(is0, f_end[core * NP + i], f_swap[i])
        second = choose(last0 == first1, e0) + choose(first0 == first1, x)
        f_give[i] = jnp.where(is0, second, x)
        f_carry[core * NP + i] = jnp.where(is0, x, second)

    f_swap_out.start()
    f_swap_out.wait_recv()

    gain = gain_ref[...]
    lane = lax.broadcasted_iota(jnp.int32, (C, 128), 1)
    stat = jnp.zeros((C, 128), F32)
    for n in range(NB):
        match = jnp.where(doc_ref[n] == doc_ref[0], 1.0, 0.0).astype(F32)
        sq = jnp.zeros((C, HD), F32)
        inn = jnp.zeros((C, HD), F32)
        for h in range(NH):
            enter = state_ref[n, piece(h)] + match * f_carry[piece(h)]
            enter = enter.reshape(HD, HD).astype(BF16)
            enter_ref[n, h] = enter
            att = att_ref[rows(n), cols(h)] + mm(q_ref[rows(n), cols(h)], enter, NN)
            att_ref[rows(n), cols(h)] = att
            sq = sq + att * att
            inn = inn + (g_ref[rows(n), cols(h)].astype(F32) * gain[:, cols(h)]) * att
        stat = jnp.where(lane == n, jnp.sum(sq, axis=1, keepdims=True), stat)
        stat = jnp.where(lane == 8 + n, jnp.sum(inn, axis=1, keepdims=True), stat)
    stat_t = jnp.transpose(stat)[0:16]
    stat_send[...] = stat_t
    stat_in[mt] = stat_t

    def t_copy(i):
        return pltpu.make_async_remote_copy(
            src_ref=stat_send,
            dst_ref=stat_in.at[mt],
            send_sem=tsend_sem.at[i],
            recv_sem=trecv_sem.at[i],
            device_id={"tp": lax.rem(mt + i, NT_)},
            device_id_type=MESH,
        )

    @pl.loop(1, NT_)
    def _(i):
        t_copy(i).start()

    wait_send(f2_copy, NP)

    @pl.loop(1, NT_)
    def _(i):
        t_copy(i).wait()

    total = stat_in[0]
    for i in range(1, NT_):
        total = total + stat_in[i]
    r = lax.rsqrt(total[0:8] / QW + epsilon)
    coef = r * r * r * (total[8:16] / QW)
    packed = jnp.concatenate([r, coef, jnp.zeros((112, C), F32)], axis=0)
    columns = jnp.transpose(packed)

    def back(first):
        for n in reversed(range(NB)):
            rc = columns[:, n : n + 1]
            cc = columns[:, 8 + n : 9 + n]
            for i in range(HH):
                h = first + i
                att = att_ref[rows(n), cols(h)]
                w = g_ref[rows(n), cols(h)].astype(F32) * gain_ref[:, cols(h)]
                d = (rc * w - att * cc).astype(BF16)
                d_ref[rows(n), cols(h)] = d
                o_norm[rows(n), cols(h)] = (att * rc * gain_ref[:, cols(h)]).astype(BF16)
                qd = mm(q_ref[rows(n), cols(h)], d, TN).reshape(HP, PR, HD)
                if n == NB - 1:
                    run = jnp.zeros((HP, PR, HD), F32)
                else:
                    run = jnp.where(same(n, n + 1) > 0.0, b_end[piece(h)], 0.0)
                leave_ref[n, piece(h)] = run
                b_end[piece(h)] = run + qd

    back(other * HH)
    b_swap_in.start()
    back(core * HH)
    b_swap_in.wait_recv()

    @pl.loop(0, NP)
    def _(i):
        own, got = b_end[core * NP + i], b_swap[i]
        e0, e1 = jnp.where(is0, own, got), jnp.where(is0, got, own)
        b_chip[i] = e0 + choose(first0 == first1, e1)

    start_all(b1_copy, NP)
    b_in[chip] = b_chip[chip]

    def outer(n):
        for h in range(NH):
            q = q_ref[rows(n), cols(h)]
            d = d_ref[rows(n), cols(h)]
            gs = mm(d, v_ref[rows(n), cols(h)], NT)
            gs = jnp.where(causal, gs, 0.0).astype(BF16)
            qg = mm(d, enter_ref[n, h], NT) + mm(gs, k_ref[rows(n), cols(h)], NN)
            o_qg[rows(n), cols(h)] = qg.astype(BF16)
            kp_ref[rows(n), cols(h)] = mm(gs, q, TN)
            vp_ref[rows(n), cols(h)] = mm(sc_ref[n * NH + h], d, TN)

    @pl.loop(0, NB // 2)
    def _(n):
        outer(n)

    wait_recv(b1_copy, NP)

    def bwd_step(t, run):
        j = NP - 1 - t
        after = jnp.minimum(j + 2, NP - 1)
        first = docs[2 * j + 2, 0:1, :]
        run = b_in[j + 1] + choose((docs[2 * after, 0:1, :] == first) & (t >= 2), run)
        b_out[j] = choose(first == docs[2 * j + 1, 1:2, :], run)
        return run

    b_out[NP - 1] = jnp.zeros((PR, HD), F32)
    lax.fori_loop(1, NP, bwd_step, jnp.zeros((PR, HD), F32))
    wait_send(b1_copy, NP)
    start_all(b2_copy, NP)
    b_carry[core * NP + chip] = b_out[chip]

    @pl.loop(NB // 2, NB)
    def _(n):
        outer(n)

    wait_recv(b2_copy, NP)

    @pl.loop(0, NP)
    def _(i):
        x = b_carry[core * NP + i]
        e1 = jnp.where(is0, b_swap[i], b_end[core * NP + i])
        second = choose(first1 == last0, e1) + choose(last1 == last0, x)
        b_give[i] = jnp.where(is0, x, second)
        b_carry[core * NP + i] = jnp.where(is0, second, x)

    b_swap_out.start()
    b_swap_out.wait_recv()

    @pl.loop(0, NB)
    def _(n):
        match = same(n, NB - 1)
        for h in range(NH):
            leave = leave_ref[n, piece(h)] + match * b_carry[piece(h)]
            low_ref[n, h] = leave.reshape(HD, HD).astype(BF16)

    wait_send(b2_copy, NP)
    for copy in (f_swap_in, f_swap_out, b_swap_in, b_swap_out):
        copy.wait_send()


def finish(
    NB, NH,
    norm_ref, qg_ref, kp_ref, vp_ref, low_ref, k_ref, v_ref,
    normed_hbm, qg_hbm, kg_hbm, vg_hbm,
    o_kg, o_vg, store_sem,
):
    def rows(n):
        return pl.ds(pl.multiple_of(n * C, C), C)

    def store(i, ref, hbm, n):
        return pltpu.make_async_copy(ref.at[rows(n)], hbm.at[rows(n)], store_sem.at[i, n])

    @pl.loop(0, NB)
    def _(n):
        store(0, norm_ref, normed_hbm, n).start()
        store(1, qg_ref, qg_hbm, n).start()

    @pl.loop(0, NB)
    def _(n):
        for h in range(NH):
            at = slice(h * HD, (h + 1) * HD)
            leave = low_ref[n, h]
            kg = kp_ref[rows(n), at] + mm(v_ref[rows(n), at], leave, NT)
            o_kg[rows(n), at] = kg.astype(BF16)
            vg = vp_ref[rows(n), at] + mm(k_ref[rows(n), at], leave, NN)
            o_vg[rows(n), at] = vg.astype(BF16)
        store(2, o_kg, kg_hbm, n).start()
        store(3, o_vg, vg_hbm, n).start()

    @pl.loop(0, NB)
    def _(n):
        store(0, norm_ref, normed_hbm, n).wait()
        store(1, qg_ref, qg_hbm, n).wait()
        store(2, o_kg, kg_hbm, n).wait()
        store(3, o_vg, vg_hbm, n).wait()


def local(NC, NT_, queries, keys, values, out_grad, gain, doc_ids):
    tok, W = queries.shape
    NB, NH = tok // C, W // HD
    PR = NH * HD // NC
    QW = W * NT_
    any_spec = pl.BlockSpec(memory_space=pl.ANY)
    vmem_spec = pl.BlockSpec(memory_space=pltpu.VMEM)
    out = jax.ShapeDtypeStruct((tok, W), BF16)
    dma = pltpu.SemaphoreType.DMA
    whole = pltpu.VMEM((NC, PR, HD), F32)
    part = pltpu.VMEM((NC // 2, PR, HD), F32)
    ring = [whole, part, part, whole, part, part, part]
    held = (
        pltpu.VMEM((tok, W), BF16),
        pltpu.VMEM((tok, W), BF16),
        pltpu.VMEM((tok, W), F32),
        pltpu.VMEM((tok, W), F32),
        pltpu.VMEM((NB, NH, HD, HD), BF16),
        pltpu.VMEM((tok, W), BF16),
        pltpu.VMEM((tok, W), BF16),
    )
    inner = pl.pallas_call(
        functools.partial(kernel, NC, NT_, NB, NH, QW),
        out_shape=held,
        in_specs=[pl.BlockSpec(memory_space=pltpu.SMEM)] + [any_spec] * 4 + [vmem_spec],
        out_specs=(vmem_spec,) * 7,
        scratch_shapes=[pltpu.VMEM((tok, W), BF16)] * 2
        + [
            pltpu.VMEM((NB * NH, C, C), BF16),
            pltpu.VMEM((tok, W), F32),
            pltpu.VMEM((tok, W), BF16),
            pltpu.VMEM((NB, NC, PR, HD), F32),
            pltpu.VMEM((NB, NH, HD, HD), BF16),
            pltpu.VMEM((NB, NC, PR, HD), F32),
        ]
        + [pltpu.VMEM((2, 128), F32), pltpu.VMEM((NC, 2, 128), F32)]
        + ring
        + ring
        + [
            pltpu.VMEM((16, C), F32),
            pltpu.VMEM((NT_, 16, C), F32),
            dma((4, NB)),
            dma((NC,)),
            dma((NC,)),
            dma((NC // 2,)),
            dma((NC // 2,)),
            dma((NC // 2,)),
            dma((NC // 2,)),
            dma((4,)),
            dma((4,)),
            dma((NT_,)),
            dma((NT_,)),
        ],
        compiler_params=pltpu.CompilerParams(
            collective_id=0, has_side_effects=True, vmem_limit_bytes=47 * 2**20
        ),
        name="packed_linear_attention",
    )(doc_ids, queries, keys, values, out_grad, gain.reshape(1, W))
    return pl.pallas_call(
        functools.partial(finish, NB, NH),
        out_shape=(out,) * 4,
        in_specs=[vmem_spec] * 7,
        out_specs=(any_spec,) * 4,
        scratch_shapes=[pltpu.VMEM((tok, W), BF16)] * 2 + [dma((4, NB))],
        compiler_params=pltpu.CompilerParams(vmem_limit_bytes=8 * 2**20),
        name="key_value_grads",
    )(*inner)


def solution(mesh):
    ctx, tp = mesh.shape["ctx"], mesh.shape["tp"]
    return jax.shard_map(
        functools.partial(local, ctx, tp),
        mesh=mesh,
        in_specs=(
            P("ctx", "tp"),
            P("ctx", "tp"),
            P("ctx", "tp"),
            P("ctx", "tp"),
            P("tp"),
            P("ctx"),
        ),
        out_specs=(P("ctx", "tp"), P("ctx", "tp"), P("ctx", "tp"), P("ctx", "tp")),
        check_vma=False,
    )
```

time: 63.9 us -> 54.3 us (0.85)
  local copies, waits for them, and re-layouts: 7.87 us -> 0 us
  Pallas kernels: 55.2 us -> 53.6 us
    unnamed x10 -> x0, local copies, waits for them, and re-layouts: 7.87 us -> none
    pallas_call x1, Pallas kernels: 55.2 us -> 50.7 us  [local(): pl.pallas_call(functools.partial(kernel, NC, NT_, NB, NH, QW), out_shape=...]
    pallas_call x0 -> x1, Pallas kernels: none -> 2.84 us  [local(): pl.pallas_call(functools.partial(finish, NB, NH), out_shape=(out,) * 4, i...]
where the time goes in v2:
time: 54.3 us; the launch traced here: 54.2 us
  Pallas kernels  53.6 us (99%)
  between operations  0.64 us (1%)
    pallas_call x1, Pallas kernels, local(): pl.pallas_call(functools.partial(kernel, NC, NT_, NB, NH, QW), out_shape=...  50.7 us
    pallas_call x1, Pallas kernels, local(): pl.pallas_call(functools.partial(finish, NB, NH), out_shape=(out,) * 4, i...  2.84 us

profile of v2, /device:TPU:1, one launch (start us, length us, event | category | flops | bytes accessed | tf_op | source)
XLA Modules:
  0.0 54.2 jit_solution(17895239468193821174)
XLA Ops:
  0.6 50.7 %packed_linear_attention.1 = (bf16[1536,512]{1,0:T(8,128)(2,1)S(1)}, bf16[1536,512]{1,0:T(8,128)(2,1)S(1)}, f32[1536,512]{1,0:T(8,128)S(1)}, f32[1536,512]{1,0:T...) custom-call(s32[6]{0:T(128)} %doc_ref.1, ...), custom_call_target="tpu_custom_call" | custom-call | tf_op jit(solution)/shard_map/packed_linear_attention/pallas_call | solution.py:472
  51.4 2.8 %key_value_grads.1 = (bf16[1536,512]{1,0:T(8,128)(2,1)}, bf16[1536,512]{1,0:T(8,128)(2,1)}, bf16[1536,512]{1,0:T(8,128)(2,1)}, bf16[1536,512]{1,0:T(8,128)(2,1)}) custom-call(bf16[1536,512]{1,0:T(8,128)(2,1)S(1)} %get-tuple-element.11.norm_ref, bf16[1536,512]{1,0:T(8,128)(2,1)S(1)} %get-tuple-element.12.qg_ref, f32[1536,512]{1,0:T(8,128)S(1)} %get-tuple-element.13.kp_ref, ...), custom_call_target="tpu_custom_call" | custom-call | tf_op jit(solution)/shard_map/key_value_grads/pallas_call | solution.py:509

commit v3 on v2

--- a/solution.py
+++ b/solution.py
@@ -1,4 +1,5 @@
 import functools
+import math
 
 import jax
 import jax.numpy as jnp
@@ -31,7 +32,7 @@
     o_norm, o_qg, kp_ref, vp_ref, low_ref, k_ref, v_ref,
     q_ref, g_ref,
     sc_ref, att_ref, d_ref, state_ref, enter_ref, leave_ref,
-    docrow, docs,
+    sq_ref, inn_ref, docrow, docs,
     f_end, f_in, f_out, f_carry, f_swap, f_chip, f_give,
     b_end, b_in, b_out, b_carry, b_swap, b_chip, b_give,
     stat_send, stat_in,
@@ -114,27 +115,42 @@
     def _(i):
         doc_copy(i).start()
 
+    side = math.isqrt(NP)
+    if side * side != NP:
+        side = 1
+
+    def to(i):
+        row = lax.rem(chip // side + i // side, NP // side)
+        return row * side + lax.rem(chip + i, side)
+
+    def far(n, i):
+        return min(i, n - i)
+
+    order = sorted(
+        range(1, NP), key=lambda i: -far(NP // side, i // side) - far(side, i % side)
+    )
+
     def chips(i, src, dst, recv):
         return pltpu.make_async_remote_copy(
             src_ref=src,
             dst_ref=dst,
             send_sem=send_sem.at[i],
             recv_sem=recv.at[i],
-            device_id={"ctx": lax.rem(chip + i, NP) * 2 + core},
+            device_id={"ctx": to(i) * 2 + core},
             device_id_type=MESH,
         )
 
     def f1_copy(i):
-        return chips(i, f_chip.at[lax.rem(chip + i, NP)], f_in.at[chip], f1_sem)
+        return chips(i, f_chip.at[to(i)], f_in.at[chip], f1_sem)
 
     def f2_copy(i):
-        return chips(i, f_out.at[lax.rem(chip + i, NP)], f_carry.at[core * NP + chip], f2_sem)
+        return chips(i, f_out.at[to(i)], f_carry.at[core * NP + chip], f2_sem)
 
     def b1_copy(i):
-        return chips(i, b_chip.at[lax.rem(chip + i, NP)], b_in.at[chip], b1_sem)
+        return chips(i, b_chip.at[to(i)], b_in.at[chip], b1_sem)
 
     def b2_copy(i):
-        return chips(i, b_out.at[lax.rem(chip + i, NP)], b_carry.at[core * NP + chip], b2_sem)
+        return chips(i, b_out.at[to(i)], b_carry.at[core * NP + chip], b2_sem)
 
     def swap(i, src, dst):
         return pltpu.make_async_remote_copy(
@@ -158,6 +174,10 @@
         def _(i):
             copy(i).start()
 
+    def start_far(copy):
+        for i in order:
+            copy(i).start()
+
     def wait_send(copy, count):
         @pl.loop(1, count)
         def _(i):
@@ -207,13 +227,11 @@
 
     f_swap_in.wait_recv()
 
-    @pl.loop(0, NP)
-    def _(i):
-        own, got = f_end[core * NP + i], f_swap[i]
-        e0, e1 = jnp.where(is0, own, got), jnp.where(is0, got, own)
-        f_chip[i] = e1 + choose(last0 == last1, e0)
-
-    start_all(f1_copy, NP)
+    own, got = f_end[mine], f_swap[...]
+    e0, e1 = jnp.where(is0, own, got), jnp.where(is0, got, own)
+    f_chip[...] = e1 + choose((last0 == last1)[None], e0)
+
+    start_far(f1_copy)
     f_in[chip] = f_chip[chip]
 
     causal = lax.broadcasted_iota(jnp.int32, (C, C), 0) >= lax.broadcasted_iota(
@@ -243,9 +261,9 @@
         return run
 
     f_out[0] = jnp.zeros((PR, HD), F32)
-    lax.fori_loop(1, NP, fwd_step, jnp.zeros((PR, HD), F32))
+    lax.fori_loop(1, NP, fwd_step, jnp.zeros((PR, HD), F32), unroll=True)
     wait_send(f1_copy, NP)
-    start_all(f2_copy, NP)
+    start_far(f2_copy)
     f_carry[core * NP + chip] = f_out[chip]
 
     @pl.loop(NB // 2, NB)
@@ -258,32 +276,34 @@
 
     wait_recv(f2_copy, NP)
 
-    @pl.loop(0, NP)
-    def _(i):
-        x = f_carry[core * NP + i]
-        e0 = jnp.where(is0, f_end[core * NP + i], f_swap[i])
-        second = choose(last0 == first1, e0) + choose(first0 == first1, x)
-        f_give[i] = jnp.where(is0, second, x)
-        f_carry[core * NP + i] = jnp.where(is0, x, second)
-
+    x = f_carry[mine]
+    e0 = jnp.where(is0, f_end[mine], f_swap[...])
+    second = choose((last0 == first1)[None], e0) + choose((first0 == first1)[None], x)
+    f_give[...] = jnp.where(is0, second, x)
     f_swap_out.start()
-    f_swap_out.wait_recv()
-
-    gain = gain_ref[...]
+    f_carry[mine] = jnp.where(is0, x, second)
+
     lane = lax.broadcasted_iota(jnp.int32, (C, 128), 1)
-    stat = jnp.zeros((C, 128), F32)
-    for n in range(NB):
+    def attend(n, first, sq, inn):
         match = jnp.where(doc_ref[n] == doc_ref[0], 1.0, 0.0).astype(F32)
-        sq = jnp.zeros((C, HD), F32)
-        inn = jnp.zeros((C, HD), F32)
-        for h in range(NH):
+        for i in range(HH):
+            h = first + i
             enter = state_ref[n, piece(h)] + match * f_carry[piece(h)]
             enter = enter.reshape(HD, HD).astype(BF16)
             enter_ref[n, h] = enter
             att = att_ref[rows(n), cols(h)] + mm(q_ref[rows(n), cols(h)], enter, NN)
             att_ref[rows(n), cols(h)] = att
             sq = sq + att * att
-            inn = inn + (g_ref[rows(n), cols(h)].astype(F32) * gain[:, cols(h)]) * att
+            inn = inn + (g_ref[rows(n), cols(h)].astype(F32) * gain_ref[:, cols(h)]) * att
+        return sq, inn
+
+    for n in range(NB):
+        zero = jnp.zeros((C, HD), F32)
+        sq_ref[rows(n)], inn_ref[rows(n)] = attend(n, core * HH, zero, zero)
+    f_swap_out.wait_recv()
+    stat = jnp.zeros((C, 128), F32)
+    for n in range(NB):
+        sq, inn = attend(n, other * HH, sq_ref[rows(n)], inn_ref[rows(n)])
         stat = jnp.where(lane == n, jnp.sum(sq, axis=1, keepdims=True), stat)
         stat = jnp.where(lane == 8 + n, jnp.sum(inn, axis=1, keepdims=True), stat)
     stat_t = jnp.transpose(stat)[0:16]
@@ -342,13 +362,11 @@
     back(core * HH)
     b_swap_in.wait_recv()
 
-    @pl.loop(0, NP)
-    def _(i):
-        own, got = b_end[core * NP + i], b_swap[i]
-        e0, e1 = jnp.where(is0, own, got), jnp.where(is0, got, own)
-        b_chip[i] = e0 + choose(first0 == first1, e1)
-
-    start_all(b1_copy, NP)
+    own, got = b_end[mine], b_swap[...]
+    e0, e1 = jnp.where(is0, own, got), jnp.where(is0, got, own)
+    b_chip[...] = e0 + choose((first0 == first1)[None], e1)
+
+    start_far(b1_copy)
     b_in[chip] = b_chip[chip]
 
     def outer(n):
@@ -377,9 +395,9 @@
         return run
 
     b_out[NP - 1] = jnp.zeros((PR, HD), F32)
-    lax.fori_loop(1, NP, bwd_step, jnp.zeros((PR, HD), F32))
+    lax.fori_loop(1, NP, bwd_step, jnp.zeros((PR, HD), F32), unroll=True)
     wait_send(b1_copy, NP)
-    start_all(b2_copy, NP)
+    start_far(b2_copy)
     b_carry[core * NP + chip] = b_out[chip]
 
     @pl.loop(NB // 2, NB)
@@ -388,23 +406,24 @@
 
     wait_recv(b2_copy, NP)
 
-    @pl.loop(0, NP)
-    def _(i):
-        x = b_carry[core * NP + i]
-        e1 = jnp.where(is0, b_swap[i], b_end[core * NP + i])
-        second = choose(first1 == last0, e1) + choose(last1 == last0, x)
-        b_give[i] = jnp.where(is0, x, second)
-        b_carry[core * NP + i] = jnp.where(is0, second, x)
-
+    x = b_carry[mine]
+    e1 = jnp.where(is0, b_swap[...], b_end[mine])
+    second = choose((first1 == last0)[None], e1) + choose((last1 == last0)[None], x)
+    b_give[...] = jnp.where(is0, x, second)
     b_swap_out.start()
+    b_carry[mine] = jnp.where(is0, second, x)
+
+    def lower(first):
+        for n in range(NB):
+            match = same(n, NB - 1)
+            for i in range(HH):
+                h = first + i
+                leave = leave_ref[n, piece(h)] + match * b_carry[piece(h)]
+                low_ref[n, h] = leave.reshape(HD, HD).astype(BF16)
+
+    lower(core * HH)
     b_swap_out.wait_recv()
-
-    @pl.loop(0, NB)
-    def _(n):
-        match = same(n, NB - 1)
-        for h in range(NH):
-            leave = leave_ref[n, piece(h)] + match * b_carry[piece(h)]
-            low_ref[n, h] = leave.reshape(HD, HD).astype(BF16)
+    lower(other * HH)
 
     wait_send(b2_copy, NP)
     for copy in (f_swap_in, f_swap_out, b_swap_in, b_swap_out):
@@ -483,6 +502,7 @@
             pltpu.VMEM((NB, NH, HD, HD), BF16),
             pltpu.VMEM((NB, NC, PR, HD), F32),
         ]
+        + [pltpu.VMEM((tok, HD), F32)] * 2
         + [pltpu.VMEM((2, 128), F32), pltpu.VMEM((NC, 2, 128), F32)]
         + ring
         + ring

time: 54.3 us -> 53.1 us (0.978)
  Pallas kernels: 53.6 us -> 52.4 us
    pallas_call x1, Pallas kernels: 50.7 us -> 49.6 us  [local(): pl.pallas_call(functools.partial(kernel, NC, NT_, NB, NH, QW), out_shape=...]
where the time goes in v3:
time: 53.1 us; the launch traced here: 53 us
  Pallas kernels  52.4 us (99%)
  between operations  0.64 us (1%)
    pallas_call x1, Pallas kernels, local(): pl.pallas_call(functools.partial(kernel, NC, NT_, NB, NH, QW), out_shape=...  49.6 us
    pallas_call x1, Pallas kernels, local(): pl.pallas_call(functools.partial(finish, NB, NH), out_shape=(out,) * 4, i...  2.84 us

profile of v3, /device:TPU:1, one launch (start us, length us, event | category | flops | bytes accessed | tf_op | source)
XLA Modules:
  0.0 53.0 jit_solution(10817128804889593582)
XLA Ops:
  0.6 49.6 %packed_linear_attention.1 = (bf16[1536,512]{1,0:T(8,128)(2,1)S(1)}, bf16[1536,512]{1,0:T(8,128)(2,1)S(1)}, f32[1536,512]{1,0:T(8,128)S(1)}, f32[1536,512]{1,0:T...) custom-call(s32[6]{0:T(128)} %doc_ref.1, ...), custom_call_target="tpu_custom_call" | custom-call | tf_op jit(solution)/shard_map/packed_linear_attention/pallas_call | solution.py:491
  50.2 2.8 %key_value_grads.1 = (bf16[1536,512]{1,0:T(8,128)(2,1)}, bf16[1536,512]{1,0:T(8,128)(2,1)}, bf16[1536,512]{1,0:T(8,128)(2,1)}, bf16[1536,512]{1,0:T(8,128)(2,1)}) custom-call(bf16[1536,512]{1,0:T(8,128)(2,1)S(1)} %get-tuple-element.11.norm_ref, bf16[1536,512]{1,0:T(8,128)(2,1)S(1)} %get-tuple-element.12.qg_ref, f32[1536,512]{1,0:T(8,128)S(1)} %get-tuple-element.13.kp_ref, ...), custom_call_target="tpu_custom_call" | custom-call | tf_op jit(solution)/shard_map/key_value_grads/pallas_call | solution.py:529
